TPU v7x, 512 devices: a whole 4x8x8 slice. The times are simulated.
512 devices in a mesh: row: 16 (over x, y_hi), col: 32 (over z, y_lo, core).
Axes of the slice: x: 4, y: 8 (y_hi: 4, y_lo: 2; y = y_hi * 2 + y_lo), z: 8, core: 2. Of those that a mesh axis runs over, the one named last changes fastest.
Arguments:
- left_factor: float32 [8192, 512], P(('row', 'col')), may hold values from -0.0625 to 0.0625
- left_cotangent: float32 [8192, 512], P(('row', 'col')), may hold values from -80 to 80
- right_factor: float32 [24576, 512], P(('col', 'row')), may hold values from -0.0390625 to 0.0390625
- right_cotangent: float32 [24576, 512], P(('col', 'row')), may hold values from -80 to 80
- singular: float32 [512], replicated, may hold values from 0.5 to 2, as said below
- singular_cotangent: float32 [512], replicated, may hold values from -384 to 384
Outputs:
- matrix_cotangent: float32 [8192, 24576], P('row', 'col')
Inputs may be any that keep to these rules, and one draw needn't show every extreme that they name: `singular`: strictly decreasing; consecutive values differ by at least 0.75 / 512.
All inputs are finite; a program needn't handle non-finite values.
Results may differ from a plain program's by a relative error of at most 0.0003.
Values sent between devices are 32-bit elements; how exact they have to be, the bound alone decides.
No kernel may reach another device: no remote copies, remote signals or barrier semaphores. Data moves between devices by JAX's collectives and lax.ppermute only.
A program may use at most 64 MiB of HBM per device.

v0:
```python
import jax
import jax.numpy as jnp
from jax import lax
from jax.sharding import PartitionSpec as P


def linear_core(gram_left, gram_right, singular):
    squares = singular * singular
    spread = squares[None, :] - squares[:, None]
    size_k = singular.shape[0]
    diagonal = jnp.eye(size_k, dtype=jnp.bool_)
    divided = jnp.where(
        diagonal, jnp.float32(0.0), 1.0 / jnp.where(diagonal, jnp.float32(1.0), spread)
    )
    inverse = 1.0 / singular
    core = divided * (gram_left - gram_left.T) * singular[None, :]
    core = core + singular[:, None] * (divided * (gram_right - gram_right.T))
    return core - gram_left * inverse[None, :] - inverse[:, None] * gram_right.T


def local(left_factor, left_cotangent, right_factor, right_cotangent, singular, singular_cotangent):
    highest = lax.Precision.HIGHEST
    dims = (((1,), (1,)), ((), ()))
    inverse = 1.0 / singular
    right_whole, right_cot_whole = (
        lax.all_gather(right_factor, "row", axis=0, tiled=True),
        lax.all_gather(right_cotangent, "row", axis=0, tiled=True),
    )
    scaled_right = right_cot_whole * inverse[None, :]
    local_left = jnp.dot(
        left_factor.T, left_cotangent, precision=highest, preferred_element_type=jnp.float32
    )
    local_right = jnp.dot(
        right_factor.T, right_cotangent, precision=highest, preferred_element_type=jnp.float32
    )
    gram_left, gram_right = lax.psum((local_left, local_right), ("row", "col"))
    core = linear_core(gram_left, gram_right, singular)
    core = core + jnp.diag(singular_cotangent)
    panel = (
        jnp.dot(left_factor, core, precision=highest, preferred_element_type=jnp.float32)
        + left_cotangent * inverse[None, :]
    )
    pieces = lax.all_gather((panel, left_factor), "col", axis=0, tiled=True)
    result = lax.dot_general(
        pieces[0], right_whole, dims, precision=highest, preferred_element_type=jnp.float32
    )
    return result + lax.dot_general(
        pieces[1], scaled_right, dims, precision=highest, preferred_element_type=jnp.float32
    )


def solution(mesh):
    placed = (
        P(("row", "col"), None),
        P(("row", "col"), None),
        P(("col", "row"), None),
        P(("col", "row"), None),
        P(),
        P(),
    )
    return jax.shard_map(
        local, mesh=mesh, in_specs=placed, out_specs=P("row", "col"), check_vma=False
    )
```

profile of v0, /device:TPU:1, one launch (start us, length us, event | category | flops | bytes accessed | tf_op | source)
XLA Modules:
  0.0 570.3 jit_solution(9918086712655896282)
XLA Ops:
  6.5 0.0 all-reduce.3.cloned.1.call-start
  6.5 2.8 fusion.31
  9.3 0.0 copy-start.4
  9.3 2.9 fusion.32
  12.3 0.0 all-reduce.3.cloned.1.call-update
  12.3 0.0 all-gather.11.cloned.1.call-start
  12.3 0.7 all-gather.11.cloned.1.call-update
  13.0 0.0 all-gather.9.cloned.1.call-start
  13.1 0.7 all-gather.9.cloned.1.call-update
  13.8 0.0 all-gather.7.cloned.1.call-start
  13.8 0.5 all-gather.7.cloned.1.call-update
  14.4 0.0 all-gather.5.cloned.1.call-start
  14.4 0.0 copy-done.4
  14.4 285.5 %all-reduce.3.cloned.1.call-done = (f32[512,512]{0,1:T(8,128)}, f32[512,512]{1,0:T(8,128)}) async-done(((f32[512,512]{0,1:T(8,128)}, f32[512,512]{1,0:T(8,128)}), (f32[512,512]{0,1:T(8,128)}, f32[512,512]{1,0:T(8,128)})) %all-reduce.3.cloned.1.call-update) | async-done | bytes 2097168 | tf_op jit(solution)/shard_map/psum | solution.py:36
  300.0 0.0 copy-start
  300.0 1.6 copy.7
  301.6 0.0 copy-start.1
  301.6 0.0 copy-start.2
  301.6 0.0 copy-start.3
  301.6 0.0 copy-start.5
  301.7 0.0 copy-done
  301.7 1.3 copy.9
  303.0 0.0 copy-done.1
  303.0 0.0 copy-done.2
  303.0 0.0 copy-done.3
  303.0 0.0 copy-done.5
  303.0 3.1 fusion.2
  306.1 0.0 all-gather.5.cloned.1.call-update
  306.1 59.1 %all-gather.11.cloned.1.call-done = f32[512,512]{1,0:T(8,128)} async-done(((f32[16,512]{1,0:T(8,128)}), f32[512,512]{1,0:T(8,128)}) %all-gather.11.cloned.1.call-update) | async-done | bytes 1048592 | tf_op jit(solution)/shard_map/all_gather | solution.py:43
  365.2 60.7 %all-gather.9.cloned.1.call-done = f32[768,512]{1,0:T(8,128)} async-done(((f32[48,512]{1,0:T(8,128)}), f32[768,512]{1,0:T(8,128)}) %all-gather.9.cloned.1.call-update) | async-done | bytes 1572880 | tf_op jit(solution)/shard_map/all_gather | solution.py:27
  425.9 4.4 fusion
  430.3 58.0 %all-gather.7.cloned.1.call-done = f32[768,512]{1,0:T(8,128)} async-done(((f32[48,512]{1,0:T(8,128)}), f32[768,512]{1,0:T(8,128)}) %all-gather.7.cloned.1.call-update) | async-done | bytes 1572880 | tf_op jit(solution)/shard_map/all_gather | solution.py:26
  488.3 69.9 %all-gather.5.cloned.1.call-done = f32[512,512]{1,0:T(8,128)} async-done(((f32[16,512]{1,0:T(8,128)}), f32[512,512]{1,0:T(8,128)}) %all-gather.5.cloned.1.call-update) | async-done | bytes 1048592 | tf_op jit(solution)/shard_map/all_gather | solution.py:43
  558.2 5.6 bitcast_add_fusion
  (1 shorter events, 0.0 us)
Async XLA Ops:
  6.5 293.4 %all-reduce.3.cloned.1.call-start = ((), (), s32[]{:S(2)}) async-start(), calls=%async_computation.4 | async-start | bytes 4194304 | tf_op jit(solution)/shard_map/psum | solution.py:36
  9.3 5.1 copy-start.4
  12.3 352.9 %all-gather.11.cloned.1.call-start = ((), (), s32[]{:S(2)}) async-start(), calls=%async_computation.3 | async-start | bytes 1081344 | tf_op jit(solution)/shard_map/all_gather | solution.py:43
  13.0 412.8 %all-gather.9.cloned.1.call-start = ((), (), s32[]{:S(2)}) async-start(), calls=%async_computation.2 | async-start | bytes 1671168 | tf_op jit(solution)/shard_map/all_gather | solution.py:27
  13.8 474.5 %all-gather.7.cloned.1.call-start = ((), (), s32[]{:S(2)}) async-start(), calls=%async_computation.1 | async-start | bytes 1671168 | tf_op jit(solution)/shard_map/all_gather | solution.py:26
  14.4 543.9 %all-gather.5.cloned.1.call-start = ((), (), s32[]{:S(2)}) async-start(), calls=%async_computation | async-start | bytes 1081344 | tf_op jit(solution)/shard_map/all_gather | solution.py:43
  300.0 1.7 copy-start
  301.6 1.4 copy-start.1
  301.6 1.4 copy-start.2
  301.6 1.3 copy-start.3
  301.6 1.3 copy-start.5
Sparse Core Ops, SparseCore 0:
  12.4 287.5 all-reduce.2
  302.1 63.0 all-gather.10
  368.3 57.5 all-gather.8
  428.8 59.4 all-gather.6
  490.3 67.9 all-gather.4
where the time goes:
time: 571 us; the launch traced here: 570 us
  waiting for transfers between devices  535 us (94%)
  matrix products  18.8 us (3%)
  between operations  13.2 us (2%)
    psum x1, waiting for transfers between devices, local(): gram_left, gram_right = lax.psum((local_left, local_right), ('row', 'col'))  286 us
    all_gather x2, waiting for transfers between devices, local(): pieces = lax.all_gather((panel, left_factor), 'col', axis=0, tiled=True)  129 us
    all_gather x1, waiting for transfers between devices, local(): lax.all_gather(right_cotangent, 'row', axis=0, tiled=True)  60.7 us
    all_gather x1, waiting for transfers between devices, local(): lax.all_gather(right_factor, 'row', axis=0, tiled=True)  58 us
  transfers between devices with their start and end apart: 5, of which 5 were waited for; matrix products, arithmetic and copies ran while one was open for 2% of the time, Pallas kernels for 0%

commit v1 on v0

--- a/solution.py
+++ b/solution.py
@@ -1,7 +1,16 @@
+import functools
 import jax
 import jax.numpy as jnp
 from jax import lax
 from jax.sharding import PartitionSpec as P
+
+
+def create_quarters_by_axis(xx, row_axis, dev_axis):
+    after = lax.psum(lax.psum(xx, row_axis), dev_axis)
+    return after
+
+
+compute_matrix = functools.partial(create_quarters_by_axis, row_axis="row", dev_axis="col")
 
 
 def linear_core(gram_left, gram_right, singular):
@@ -33,7 +42,7 @@
     local_right = jnp.dot(
         right_factor.T, right_cotangent, precision=highest, preferred_element_type=jnp.float32
     )
-    gram_left, gram_right = lax.psum((local_left, local_right), ("row", "col"))
+    gram_left, gram_right = compute_matrix((local_left, local_right))
     core = linear_core(gram_left, gram_right, singular)
     core = core + jnp.diag(singular_cotangent)
     panel = (

time: 571 us -> 716 us (1.25)
  waiting for transfers between devices: 535 us -> 680 us
    psum x1 -> x2, waiting for transfers between devices: 286 us -> 427 us  [create_quarters_by_axis(): after = lax.psum(lax.psum(xx, row_axis), dev_axis)]
  transfers between devices with their start and end apart: 5 -> 6, of which waited for: 5 -> 6; matrix products, arithmetic and copies ran while one was open for 2% -> 1% of each run, Pallas kernels for 0% -> 0%
where the time goes in v1:
time: 716 us; the launch traced here: 715 us
  waiting for transfers between devices  680 us (95%)
  matrix products  18.8 us (3%)
  between operations  13.6 us (2%)
    psum x2, waiting for transfers between devices, create_quarters_by_axis(): after = lax.psum(lax.psum(xx, row_axis), dev_axis)  427 us
    all_gather x2, waiting for transfers between devices, local(): pieces = lax.all_gather((panel, left_factor), 'col', axis=0, tiled=True)  133 us
    all_gather x1, waiting for transfers between devices, local(): lax.all_gather(right_cotangent, 'row', axis=0, tiled=True)  60.5 us
    all_gather x1, waiting for transfers between devices, local(): lax.all_gather(right_factor, 'row', axis=0, tiled=True)  57.9 us
  transfers between devices with their start and end apart: 6, of which 6 were waited for; matrix products, arithmetic and copies ran while one was open for 1% of the time, Pallas kernels for 0%

profile of v1, /device:TPU:1, one launch (start us, length us, event | category | flops | bytes accessed | tf_op | source)
XLA Modules:
  0.0 715.5 jit_solution(16028343742845616542)
XLA Ops:
  6.5 0.0 all-reduce.7.cloned.1.call-start
  6.5 2.8 fusion.31
  9.3 2.9 fusion.32
  12.3 0.0 all-reduce.7.cloned.1.call-update
  12.3 0.0 copy-start.4
  12.3 0.0 all-reduce.5.cloned.1.call-start
  12.3 180.8 %all-reduce.7.cloned.1.call-done = (f32[512,512]{0,1:T(8,128)}, f32[512,512]{1,0:T(8,128)}) async-done(((f32[512,512]{0,1:T(8,128)}, f32[512,512]{1,0:T(8,128)}), (f32[512,512]{0,1:T(8,128)}, f32[512,512]{1,0:T(8,128)})) %all-reduce.7.cloned.1.call-update) | async-done | bytes 2097168 | tf_op jit(solution)/shard_map/psum | solution.py:9
  193.2 0.0 all-reduce.5.cloned.1.call-update
  193.2 0.0 all-gather.11.cloned.1.call-start
  193.3 0.7 all-gather.11.cloned.1.call-update
  194.0 0.0 all-gather.9.cloned.1.call-start
  194.0 0.5 all-gather.9.cloned.1.call-update
  194.5 0.0 all-gather.7.cloned.1.call-start
  194.6 0.5 all-gather.7.cloned.1.call-update
  195.1 0.0 all-gather.5.cloned.1.call-start
  195.2 0.0 copy-done.4
  195.2 246.1 %all-reduce.5.cloned.1.call-done = (f32[512,512]{0,1:T(8,128)}, f32[512,512]{1,0:T(8,128)}) async-done(((f32[512,512]{0,1:T(8,128)}, f32[512,512]{1,0:T(8,128)}), (f32[512,512]{0,1:T(8,128)}, f32[512,512]{1,0:T(8,128)})) %all-reduce.5.cloned.1.call-update) | async-done | bytes 2097168 | tf_op jit(solution)/shard_map/psum | solution.py:9
  441.3 0.0 copy-start
  441.3 1.6 copy.7
  442.9 0.0 copy-start.1
  442.9 0.0 copy-start.2
  442.9 0.0 copy-start.3
  443.0 0.0 copy-start.5
  443.0 0.0 copy-done
  443.0 1.3 copy.9
  444.3 0.0 copy-done.1
  444.3 0.0 copy-done.2
  444.3 0.0 copy-done.3
  444.3 0.0 copy-done.5
  444.3 3.1 fusion.2
  447.4 0.0 all-gather.5.cloned.1.call-update
  447.4 62.8 %all-gather.11.cloned.1.call-done = f32[512,512]{1,0:T(8,128)} async-done(((f32[16,512]{1,0:T(8,128)}), f32[512,512]{1,0:T(8,128)}) %all-gather.11.cloned.1.call-update) | async-done | bytes 1048592 | tf_op jit(solution)/shard_map/all_gather | solution.py:52
  510.2 60.5 %all-gather.9.cloned.1.call-done = f32[768,512]{1,0:T(8,128)} async-done(((f32[48,512]{1,0:T(8,128)}), f32[768,512]{1,0:T(8,128)}) %all-gather.9.cloned.1.call-update) | async-done | bytes 1572880 | tf_op jit(solution)/shard_map/all_gather | solution.py:36
  570.7 4.4 fusion
  575.1 57.9 %all-gather.7.cloned.1.call-done = f32[768,512]{1,0:T(8,128)} async-done(((f32[48,512]{1,0:T(8,128)}), f32[768,512]{1,0:T(8,128)}) %all-gather.7.cloned.1.call-update) | async-done | bytes 1572880 | tf_op jit(solution)/shard_map/all_gather | solution.py:35
  633.1 70.0 %all-gather.5.cloned.1.call-done = f32[512,512]{1,0:T(8,128)} async-done(((f32[16,512]{1,0:T(8,128)}), f32[512,512]{1,0:T(8,128)}) %all-gather.5.cloned.1.call-update) | async-done | bytes 1048592 | tf_op jit(solution)/shard_map/all_gather | solution.py:52
  703.0 5.6 bitcast_add_fusion
  (1 shorter events, 0.0 us)
Async XLA Ops:
  6.5 186.7 %all-reduce.7.cloned.1.call-start = ((), (), s32[]{:S(2)}) async-start(), calls=%async_computation.5 | async-start | bytes 4194304 | tf_op jit(solution)/shard_map/psum | solution.py:9
  12.3 182.9 %copy-start.4 = (f32[512]{0:T(512)S(1)}, f32[512]{0:T(512)}, u32[]{:S(2)}) copy-start(f32[512]{0:T(512)} %param.10) | copy-start | bytes 6148
  12.3 429.0 %all-reduce.5.cloned.1.call-start = ((), (), s32[]{:S(2)}) async-start(), calls=%async_computation.4 | async-start | bytes 4194304 | tf_op jit(solution)/shard_map/psum | solution.py:9
  193.2 317.0 %all-gather.11.cloned.1.call-start = ((), (), s32[]{:S(2)}) async-start(), calls=%async_computation.3 | async-start | bytes 1081344 | tf_op jit(solution)/shard_map/all_gather | solution.py:52
  194.0 376.7 %all-gather.9.cloned.1.call-start = ((), (), s32[]{:S(2)}) async-start(), calls=%async_computation.2 | async-start | bytes 1671168 | tf_op jit(solution)/shard_map/all_gather | solution.py:36
  194.5 438.5 %all-gather.7.cloned.1.call-start = ((), (), s32[]{:S(2)}) async-start(), calls=%async_computation.1 | async-start | bytes 1671168 | tf_op jit(solution)/shard_map/all_gather | solution.py:35
  195.1 507.9 %all-gather.5.cloned.1.call-start = ((), (), s32[]{:S(2)}) async-start(), calls=%async_computation | async-start | bytes 1081344 | tf_op jit(solution)/shard_map/all_gather | solution.py:52
  441.3 1.7 copy-start
  442.9 1.4 copy-start.1
  442.9 1.4 copy-start.2
  442.9 1.3 copy-start.3
  443.0 1.3 copy-start.5
Sparse Core Ops, SparseCore 0:
  12.4 180.7 all-reduce.6
  196.2 245.0 all-reduce.4
  443.4 66.6 all-gather.10
  513.1 57.5 all-gather.8
  573.6 59.4 all-gather.6
  635.1 67.9 all-gather.4
